TPU v7x, 256 devices: a whole 4x4x8 slice. The times are simulated.
256 devices in a mesh: gx: 32 (over z_hi, x, y), gy: 2 (over core), gz: 4 (over z_lo).
Axes of the slice: x: 4, y: 4, z: 8 (z_hi: 2, z_lo: 4; z = z_hi * 4 + z_lo), core: 2. Of those that a mesh axis runs over, the one named last changes fastest.
Arguments:
- flow_state: float32 [4, 128, 64, 512], P(None, 'gx', 'gy', 'gz'), may hold values from -6 to 6
- viscosity: float32 [4, 128, 64, 512], P(None, 'gx', 'gy', 'gz'), may hold values from 0.05 to 0.5
- lift_weight: float32 [8, 128], replicated, may hold values from -6 to 6
- lift_bias: float32 [128], replicated, may hold values from -2 to 2
- norm_gains: float32 [6, 128], replicated, may hold values from 0.1 to 1.9
- query_weight: bfloat16 [2, 128, 128], replicated, may hold values from -4 to 4
- key_weight: bfloat16 [2, 128, 128], replicated, may hold values from -4 to 4
- value_weight: bfloat16 [2, 128, 128], replicated, may hold values from -0.5 to 0.5
- output_weight: bfloat16 [2, 128, 128], replicated, may hold values from -0.5 to 0.5
- up_weight: bfloat16 [2, 128, 512], replicated, may hold values from -0.5 to 0.5
- down_weight: bfloat16 [2, 512, 128], replicated, may hold values from -0.25 to 0.25
- head_weight: bfloat16 [128, 4], replicated, may hold values from -1.5 to 1.5
Outputs:
- state_next: float32 [4, 128, 64, 512], P(None, 'gx', 'gy', 'gz')
- eddy_field: float32 [4, 128, 64, 512], P(None, 'gx', 'gy', 'gz')
All inputs are finite; a program needn't handle non-finite values.
Results may differ from a plain program's by a relative error of at most 0.0058.
The roundings to bfloat16 on the way count: a program that leaves them out, or rounds other values in their place, can miss the bound.
Values may be sent and summed in bfloat16 or wider, within the bound.
A program may use at most 64 MiB of HBM per device.

v0:
```python
import functools
import math

import jax
import jax.numpy as jnp
from jax import lax
from jax.experimental import pallas as pl
from jax.experimental.pallas import tpu as pltpu
from jax.sharding import PartitionSpec as P

EPSILON = 1e-06
TIME_STEP = 0.3
MESH = pl.DeviceIdType.MESH
F32 = jnp.float32
BF16 = jnp.bfloat16
DMA = pltpu.SemaphoreType.DMA
HIGHEST = lax.Precision.HIGHEST


def iota(shape, dim):
    return lax.broadcasted_iota(jnp.int32, shape, dim)


def rms(values, gain):
    square = jnp.mean(values * values, axis=-1, keepdims=True)
    return values * lax.rsqrt(square + EPSILON) * gain


def gelu(values):
    inner = math.sqrt(2.0 / math.pi) * (values + 0.044715 * (values * values * values))
    return 0.5 * values * (1.0 + jnp.tanh(inner))


def dot(left, right):
    return jnp.dot(left, right, preferred_element_type=F32)


def dot_nt(left, right, precision=None):
    return lax.dot_general(
        left, right, (((1,), (1,)), ((), ())), precision=precision, preferred_element_type=F32
    )


def order4(step):
    return lax.rem(2 + 3 * step + 3 * (step // 2) + 2 * (step // 3), 4)


def peer(step, gx, gy):
    tz = lax.rem(gx // 16 + 1 + step // 32, 2)
    tx = lax.rem(lax.rem(gx // 4, 4) + order4(lax.rem(step // 8, 4)), 4)
    ty = lax.rem(lax.rem(gx, 4) + order4(lax.rem(step // 2, 4)), 4)
    tc = lax.rem(gy + 1 + lax.rem(step, 2), 2)
    return tz * 16 + tx * 4 + ty, tc


def mixer(carried, mask, gains, weights):
    groups, rows, width = carried.shape
    query, key, value, out, up, down = weights
    flat = carried.reshape(groups * rows, width)
    normed = rms(flat, gains[0]).astype(BF16)
    queries = dot(normed, query).astype(BF16)
    keys = dot(normed, key).astype(BF16)
    values = dot(normed, value).astype(BF16)
    pieces = []
    for g in range(groups):
        part = slice(g * rows, (g + 1) * rows)
        scores = dot_nt(queries[part], keys[part]) * (width**-0.5)
        scores = jnp.where(mask, scores, -1e30)
        exponent = jnp.exp(scores - jnp.max(scores, axis=-1, keepdims=True))
        attention = exponent * (1.0 / jnp.sum(exponent, axis=-1, keepdims=True))
        pieces.append(dot(attention.astype(BF16), values[part]).astype(BF16))
    attended = jnp.concatenate(pieces, axis=0) if groups > 1 else pieces[0]
    residual = flat + dot(attended, out)
    again = rms(residual, gains[1]).astype(BF16)
    hidden = gelu(dot(again, up)).astype(BF16)
    return (residual + dot(hidden, down)).astype(BF16)


def main_kernel(
    state_hbm, visc_hbm, lift_hbm, bias_hbm, gains_hbm, query_hbm, key_hbm, value_hbm, out_hbm,
    up_hbm, down_hbm, head_hbm,
    next_hbm, coarse_hbm,
    s0, s1, s2, s3, visc, nu_f, nu_b, nu_sum, xs, xr, ys, yr, zs, zr, pool, filt, recv, hid, cbuf,
    ebuf, lift_w, bias_w, gains_w, query_w, key_w, value_w, out_w, up_w, down_w, head_w,
    load_sem, weight_sem, face_send, face_recv, a_send, a_recv, b_send, b_recv, edge_send, out_sem,
):
    gx, gy, gz = lax.axis_index("gx"), lax.axis_index("gy"), lax.axis_index("gz")
    plane = gx * 2 + gy
    loads = []
    for x in range(4):
        for n, (src, dst) in enumerate(((state_hbm, s0), (visc_hbm, visc))):
            loads.append(pltpu.make_async_copy(src.at[:, x], dst.at[x], load_sem.at[n, x]))
            loads[-1].start()
    weight_pairs = (
        (lift_hbm, lift_w), (bias_hbm, bias_w), (gains_hbm, gains_w), (query_hbm, query_w),
        (key_hbm, key_w), (value_hbm, value_w), (out_hbm, out_w), (up_hbm, up_w),
        (down_hbm, down_w), (head_hbm, head_w),
    )
    weight_loads = []
    for n, (src, dst) in enumerate(weight_pairs):
        weight_loads.append(pltpu.make_async_copy(src, dst, weight_sem.at[n]))
        weight_loads[-1].start()

    barrier = pltpu.get_barrier_semaphore()

    def greet(step, carry):
        tx, ty = peer(step, gx, gy)
        pl.semaphore_signal(barrier, inc=1, device_id={"gx": tx, "gy": ty}, device_id_type=MESH)
        return carry

    z_next, z_last = lax.rem(gz + 1, 4), lax.rem(gz + 3, 4)
    lax.fori_loop(0, 63, greet, 0)
    for target in (z_next, z_last):
        pl.semaphore_signal(barrier, inc=1, device_id={"gz": target}, device_id_type=MESH)
    pl.semaphore_signal(
        barrier, inc=1, device_id={"gx": 0, "gy": 0, "gz": z_next}, device_id_type=MESH
    )
    pl.semaphore_signal(
        barrier, inc=1, device_id={"gx": 31, "gy": 1, "gz": z_last}, device_id_type=MESH
    )

    for copy in loads:
        copy.wait()

    lanes32 = iota((32, 128), 1)

    def stage(e, source):
        xs[e, 0] = source[0].astype(BF16)
        xs[e, 1] = source[3].astype(BF16)
        packed = jnp.zeros((32, 128), F32)
        for x in range(4):
            for f in range(4):
                j = x * 4 + f
                ys[e, 0, j : j + 1, :] = source[x, f, 0:1, :]
                ys[e, 1, j : j + 1, :] = source[x, f, 31:32, :]
                block = source[x, f]
                packed = jnp.where(lanes32 == j, block[:, 0:1], packed)
                packed = jnp.where(lanes32 == 16 + j, block[:, 127:128], packed)
        zs[e] = packed

    x_next, x_last = lax.rem(gx + 1, 32), lax.rem(gx + 31, 32)

    def face_copies(e):
        pairs = (
            (xs.at[e, 1], xr.at[e, 0], {"gx": x_next}),
            (xs.at[e, 0], xr.at[e, 1], {"gx": x_last}),
            (zs.at[e], zr.at[e, 0], {"gz": z_next}),
            (zs.at[e], zr.at[e, 1], {"gz": z_last}),
            (ys.at[e], yr.at[e], {"gy": 1 - gy}),
        )
        return [
            pltpu.make_async_remote_copy(
                src_ref=src, dst_ref=dst, send_sem=face_send.at[e, n], recv_sem=face_recv.at[e, n],
                device_id=device, device_id_type=MESH,
            )
            for n, (src, dst, device) in enumerate(pairs)
        ]

    stage(0, s0)
    stage(1, visc)
    extra = jnp.where(plane == 0, 64, 0) + jnp.where(plane == 63, 64, 0)
    pl.semaphore_wait(barrier, 65 + extra)
    copies = [face_copies(e) for e in range(4)]
    for e in range(2):
        for copy in copies[e]:
            copy.start()

    rows = iota((128, 128), 0)
    lanes = iota((128, 128), 1)
    row32 = lax.rem(rows, 32)

    def neighbours(e, source, x):
        middle = source[x].reshape(128, 128)
        if x == 0:
            x_b = xr[e, 0].astype(F32).reshape(128, 128)
        else:
            x_b = source[x - 1].reshape(128, 128)
        if x == 3:
            x_f = xr[e, 1].astype(F32).reshape(128, 128)
        else:
            x_f = source[x + 1].reshape(128, 128)

        def spread(side):
            return jnp.concatenate(
                [
                    jnp.broadcast_to(yr[e, side, x * 4 + f : x * 4 + f + 1, :], (32, 128))
                    for f in range(4)
                ],
                axis=0,
            )

        y_b = jnp.where(row32 == 0, spread(1), pltpu.roll(middle, 1, 0))
        y_f = jnp.where(row32 == 31, spread(0), pltpu.roll(middle, 127, 0))

        def column(side, first):
            return jnp.concatenate(
                [
                    jnp.broadcast_to(
                        zr[e, side, :, first + x * 4 + f : first + x * 4 + f + 1], (32, 128)
                    )
                    for f in range(4)
                ],
                axis=0,
            )

        z_b = jnp.where(lanes == 0, column(0, 16), pltpu.roll(middle, 1, 1))
        z_f = jnp.where(lanes == 127, column(1, 0), pltpu.roll(middle, 127, 1))
        return middle, ((x_b, x_f), (y_b, y_f), (z_b, z_f))

    def advance(e, source, combine):
        for x in range(4):
            middle, pairs = neighbours(e, source, x)
            total = -middle * nu_sum[x]
            for d, (before, after) in enumerate(pairs):
                half = (0.5 * TIME_STEP) * source[x, d]
                half = jnp.concatenate([half] * 4, axis=0)
                total += after * (nu_f[d, x] - half) + before * (nu_b[d, x] + half)
            combine(x, middle + total)

    for copy in copies[1]:
        copy.wait_recv()
    for x in range(4):
        middle, pairs = neighbours(1, visc, x)
        total = jnp.zeros((128, 128), F32)
        for d, (before, after) in enumerate(pairs):
            forward = (0.5 * TIME_STEP) * (middle + after)
            backward = (0.5 * TIME_STEP) * (middle + before)
            nu_f[d, x] = forward
            nu_b[d, x] = backward
            total += forward + backward
        nu_sum[x] = total

    def first(x, value):
        s1[x] = value.reshape(4, 32, 128)

    def second(x, value):
        s2[x] = (0.75 * s0[x].reshape(128, 128) + 0.25 * value).reshape(4, 32, 128)

    def third(x, value):
        s3[x] = (s0[x].reshape(128, 128) / 3.0 + (2.0 / 3.0) * value).reshape(4, 32, 128)

    for copy in copies[0]:
        copy.wait_recv()
    advance(0, s0, first)
    stage(2, s1)
    for copy in copies[2]:
        copy.start()
    for copy in copies[2]:
        copy.wait_recv()
    advance(2, s1, second)
    stage(3, s2)
    for copy in copies[3]:
        copy.start()
    for copy in copies[3]:
        copy.wait_recv()
    advance(3, s2, third)

    results = []
    for x in range(4):
        results.append(pltpu.make_async_copy(s3.at[x], next_hbm.at[:, x], out_sem.at[x]))
        results[-1].start()

    pick = jnp.where(iota((64, 128), 1) // 2 == iota((64, 128), 0), 0.125, 0.0)
    for x in range(2):
        one, two = s3[2 * x].reshape(128, 128), s3[2 * x + 1].reshape(128, 128)
        pool[x, 0:128] = one + two
        pool[x, 128:256] = one * one + two * two
        paired = pool[x, pl.ds(0, 128, stride=2), :] + pool[x, pl.ds(1, 128, stride=2), :]
        filt[:, x, :] = dot_nt(pick, paired, HIGHEST)

    def send_filtered(step, carry):
        tx, ty = peer(step, gx, gy)
        pltpu.make_async_remote_copy(
            src_ref=filt.at[tx * 2 + ty], dst_ref=recv.at[gy * 32 + gx], send_sem=a_send,
            recv_sem=a_recv, device_id={"gx": tx, "gy": ty}, device_id_type=MESH,
        ).start()
        return carry

    lax.fori_loop(0, 63, send_filtered, 0)
    recv[pl.ds(gy * 32 + gx, 1)] = filt[pl.ds(plane, 1)]

    for copy in weight_loads:
        copy.wait()
    lift_rows = jnp.concatenate(
        [jnp.broadcast_to(lift_w[c : c + 1, :], (16, 128)) for c in range(8)], axis=0
    )
    head_lanes = jnp.concatenate(
        [jnp.broadcast_to(head_w[:, f : f + 1].astype(F32), (128, 32)) for f in range(4)], axis=1
    ).astype(BF16)

    a_all = pltpu.make_async_remote_copy(
        src_ref=filt.at[pl.ds(0, 63)], dst_ref=recv.at[pl.ds(0, 63)], send_sem=a_send,
        recv_sem=a_recv, device_id={"gy": 1 - gy}, device_id_type=MESH,
    )
    a_all.wait_recv()

    filtered = jnp.concatenate([recv[:, 0, :], recv[:, 1, :]], axis=0)
    along_x = lax.rem(rows // 32, 2) == lax.rem(lanes // 32, 2)
    lane16 = lax.rem(lanes, 16)

    def block_weights(i):
        return (query_w[i], key_w[i], value_w[i], out_w[i], up_w[i], down_w[i])

    def gain(i):
        return gains_w[i : i + 1, :]

    GROUP = 4

    def x_block(step, carry):
        inputs = jnp.concatenate(
            [jnp.where(lane16 == step * GROUP + g, filtered, 0.0) for g in range(GROUP)], axis=0
        )
        lifted = (
            jnp.dot(inputs, lift_rows, precision=HIGHEST, preferred_element_type=F32) + bias_w[...]
        )
        features = gelu(rms(lifted, gain(0))).astype(BF16).astype(F32)
        result = mixer(
            features.reshape(GROUP, 128, 128), along_x, (gain(1), gain(2)), block_weights(0)
        )
        hid[pl.ds(step * GROUP, GROUP)] = result.astype(F32).reshape(GROUP, 2, 2, 32, 128)
        return carry

    lax.fori_loop(0, 16 // GROUP, x_block, 0)

    along_y = lax.rem(iota((256, 256), 0), 8) == lax.rem(iota((256, 256), 1), 8)
    cell = iota((32, 8, 128), 0)
    own_lane = lax.rem(iota((32, 8, 128), 2), 32) == lax.rem(cell, 2) * 16 + cell // 2

    def y_block(x, g):
        lines = hid[:, x, :, 8 * g : 8 * g + 8, :].reshape(1, 256, 128)
        result = mixer(lines, along_y, (gain(3), gain(4)), block_weights(1))
        final = rms(result.astype(F32), gain(5)).astype(BF16)
        spread = dot(final, head_lanes).reshape(32, 8, 128)
        logits = jnp.sum(jnp.where(own_lane, spread, 0.0), axis=0)
        coefficient = 0.05 + 0.45 * (1.0 / (1.0 + jnp.exp(-logits)))
        for r in range(8):
            cbuf[1 + x + 2 * (8 * g + r)] = coefficient[r : r + 1, :]

    for x in range(2):
        for g in range(4):
            y_block(x, g)
    cbuf[0] = cbuf[64]
    cbuf[65] = cbuf[1]

    def send_coarse(step, carry):
        tx, ty = peer(step, gx, gy)
        pltpu.make_async_remote_copy(
            src_ref=cbuf.at[pl.ds(2 * tx, 4)], dst_ref=ebuf.at[plane + 1], send_sem=b_send,
            recv_sem=b_recv, device_id={"gx": tx, "gy": ty}, device_id_type=MESH,
        ).start()
        return carry

    def send_edge(slot, target_z, step, carry):
        tx, ty = peer(step, gx, gy)
        pltpu.make_async_remote_copy(
            src_ref=cbuf.at[pl.ds(2 * tx, 4)], dst_ref=ebuf.at[slot], send_sem=edge_send,
            recv_sem=b_recv, device_id={"gx": tx, "gy": ty, "gz": target_z}, device_id_type=MESH,
        ).start()
        return carry

    @pl.when(plane == 63)
    def _():
        lax.fori_loop(0, 64, functools.partial(send_edge, 0, z_next), 0)

    @pl.when(plane == 0)
    def _():
        lax.fori_loop(0, 64, functools.partial(send_edge, 65, z_last), 0)

    lax.fori_loop(0, 63, send_coarse, 0)
    ebuf[pl.ds(plane + 1, 1)] = cbuf[pl.ds(2 * gx, 4)].reshape(1, 4, 1, 128)
    ebuf[66:72] = jnp.zeros((6, 4, 1, 128), F32)
    b_all = pltpu.make_async_remote_copy(
        src_ref=ebuf.at[pl.ds(0, 63)], dst_ref=ebuf.at[pl.ds(0, 65)], send_sem=b_send,
        recv_sem=b_recv, device_id={"gy": 1 - gy}, device_id_type=MESH,
    )
    b_all.wait_recv()
    final_copy = pltpu.make_async_copy(ebuf, coarse_hbm, out_sem.at[4])
    final_copy.start()
    for e in range(4):
        for copy in copies[e]:
            copy.wait_send()
    a_all.wait_send()
    b_all.wait_send()

    @pl.when((plane == 63) | (plane == 0))
    def _():
        pltpu.make_async_remote_copy(
            src_ref=ebuf.at[pl.ds(0, 64)], dst_ref=ebuf.at[pl.ds(0, 64)], send_sem=edge_send,
            recv_sem=b_recv, device_id={"gy": 1 - gy}, device_id_type=MESH,
        ).wait_send()

    for copy in results:
        copy.wait()
    final_copy.wait()


def refine_kernel(next_in, coarse, next_out, eddy, sem):
    copy = pltpu.make_async_copy(next_in, next_out, sem)
    copy.start()
    gy = lax.axis_index("gy")
    row, column = iota((128, 128), 0), iota((128, 128), 1)
    fine = lax.rem(column, 32)
    centre = gy * 16 + fine // 2
    other = lax.rem(centre + 31 + 2 * lax.rem(fine, 2), 32)
    same = row // 32 == column // 32
    along_y = jnp.where(same & (lax.rem(row, 32) == centre), 0.75, 0.0) + jnp.where(
        same & (lax.rem(row, 32) == other), 0.25, 0.0
    )
    row, column = iota((72, 128), 0), iota((72, 128), 1)
    centre = 1 + column // 2
    other = centre - 1 + 2 * lax.rem(column, 2)
    along_z = jnp.where(row == centre, 0.75, 0.0) + jnp.where(row == other, 0.25, 0.0)
    cells = [coarse[:, x, 0, :] for x in range(4)]
    for x in range(4):
        centre, other = (1, 0, 1, 2, 2, 1, 2, 3)[2 * x : 2 * x + 2]
        mixed = 0.75 * cells[centre] + 0.25 * cells[other]
        wide = jnp.dot(mixed, along_y, precision=HIGHEST, preferred_element_type=F32)
        full = lax.dot_general(
            wide, along_z, (((0,), (0,)), ((), ())), precision=HIGHEST, preferred_element_type=F32
        )
        eddy[:, x] = full.reshape(4, 32, 128)
    copy.wait()


def per_device(state, visc, lift, bias, gains, query, key, value, out, up, down, head):
    hbm = pl.BlockSpec(memory_space=pl.ANY)
    vmem = pltpu.VMEM
    block = (4, 4, 32, 128)
    weights = (lift, bias.reshape(1, 128), gains, query, key, value, out, up, down, head)
    state_next, coarse = pl.pallas_call(
        main_kernel,
        out_shape=(
            jax.ShapeDtypeStruct(block, F32),
            jax.ShapeDtypeStruct((72, 4, 1, 128), F32),
        ),
        in_specs=[hbm] * 12,
        out_specs=(hbm, hbm),
        scratch_shapes=[vmem(block, F32)] * 5
        + [
            vmem((3, 4, 128, 128), F32),
            vmem((3, 4, 128, 128), F32),
            vmem((4, 128, 128), F32),
            vmem((4, 2, 4, 32, 128), BF16),
            vmem((4, 2, 4, 32, 128), BF16),
            vmem((4, 2, 16, 128), F32),
            vmem((4, 2, 16, 128), F32),
            vmem((4, 32, 128), F32),
            vmem((4, 2, 32, 128), F32),
            vmem((2, 256, 128), F32),
            vmem((64, 2, 128), F32),
            vmem((64, 2, 128), F32),
            vmem((16, 2, 2, 32, 128), F32),
            vmem((66, 1, 128), F32),
            vmem((72, 4, 1, 128), F32),
        ]
        + [vmem(w.shape, w.dtype) for w in weights]
        + [
            DMA((2, 4)),
            DMA((10,)),
            DMA((4, 5)),
            DMA((4, 5)),
            DMA,
            DMA,
            DMA,
            DMA,
            DMA,
            DMA((5,)),
        ],
        compiler_params=pltpu.CompilerParams(
            collective_id=0, has_side_effects=True, vmem_limit_bytes=48 << 20
        ),
        name="flow_and_columns",
    )(state, visc, *weights)
    return pl.pallas_call(
        refine_kernel,
        out_shape=(jax.ShapeDtypeStruct(block, F32), jax.ShapeDtypeStruct(block, F32)),
        in_specs=[hbm, pl.BlockSpec(memory_space=pltpu.VMEM)],
        out_specs=(hbm, pl.BlockSpec(memory_space=pltpu.VMEM)),
        scratch_shapes=[DMA],
        name="refine",
    )(state_next, coarse)


def solution(mesh):
    cells = P(None, "gx", "gy", "gz")
    return jax.shard_map(
        per_device,
        mesh=mesh,
        in_specs=(cells, cells) + (P(),) * 10,
        out_specs=(cells, cells),
        check_vma=False,
    )
```

profile of v0, /device:TPU:1, one launch (start us, length us, event | category | flops | bytes accessed | tf_op | source)
XLA Modules:
  0.0 103.1 jit_solution(16218464829945519157)
XLA Ops:
  0.6 0.0 copy-start.13
  0.6 0.7 copy-done.13
  1.3 0.0 copy-start.10
  1.3 0.0 copy-start.11
  1.3 0.1 copy.14.head_hbm
  1.5 0.5 copy-done.10
  2.0 0.0 copy-done.11
  2.0 0.0 copy-done.12
  2.0 0.0 copy-start
  2.0 0.9 copy-done
  3.0 0.0 copy-start.1
  3.0 0.9 copy-done.1
  3.9 0.0 copy-start.2
  3.9 0.9 copy-done.2
  4.9 0.9 copy-done.3
  5.8 0.8 copy-done.6
  6.7 0.8 copy-done.7
  7.5 0.8 copy-done.8
  8.3 0.8 copy-done.9
  9.2 81.9 %flow_and_columns.1 = (f32[4,4,32,128]{3,2,1,0:T(8,128)S(1)}, f32[72,4,1,128]{3,2,1,0:T(1,128)S(1)}) custom-call(f32[4,4,32,128]{3,2,1,0:T(8,128)S(1)} %copy-done, f32[4,4,32,128]{3,2,1,0:T(8,128)S(1)} %copy-done.1, f32[8,128]{1,0:T(8,128)S(1)} %copy-done.10, f32[1,128]{1,0:T(1,128)S(1)} %bitcast.1, f32[6,128]{1,0:T(8,128)S(1)} %copy-done.11, ...), custom_call_target="tpu_custom_call" | custom-call | tf_op jit(solution)/shard_map/flow_and_columns/pallas_call | solution.py:430
  91.1 0.0 copy-start.4
  91.1 0.7 copy-done.4
  91.8 0.7 copy-done.5
  92.4 10.7 %refine.1 = (f32[4,4,32,128]{3,2,1,0:T(8,128)}, f32[4,4,32,128]{3,2,1,0:T(8,128)}) custom-call(f32[4,4,32,128]{3,2,1,0:T(8,128)} %copy-done.4, f32[72,4,1,128]{3,2,1,0:T(1,128)} %copy-done.5), custom_call_target="tpu_custom_call" | custom-call | tf_op jit(solution)/shard_map/refine/pallas_call | solution.py:474
  (7 shorter events, 0.0 us)
Async XLA Ops:
  0.6 0.7 copy-start.13
  1.3 0.7 copy-start.10
  1.3 0.7 copy-start.11
  1.3 0.7 copy-start.12
  2.0 1.0 copy-start
  3.0 0.9 copy-start.1
  3.9 0.9 copy-start.2
  4.9 0.9 copy-start.3
  5.8 0.8 copy-start.6
  6.7 0.8 copy-start.7
  7.5 0.8 copy-start.8
  8.3 0.8 copy-start.9
  91.1 0.7 copy-start.4
  91.8 0.7 copy-start.5
where the time goes:
time: 104 us; the launch traced here: 103 us
  Pallas kernels  92.6 us (89%)
  local copies, waits for them, and re-layouts  9.88 us (10%)
    pallas_call x1, Pallas kernels, per_device(): pl.pallas_call(main_kernel, out_shape=(jax.ShapeDtypeStruct(block, F32),...  81.9 us
    pallas_call x1, Pallas kernels, per_device(): pl.pallas_call(refine_kernel, out_shape=(jax.ShapeDtypeStruct(block, F32)...  10.7 us
    unnamed x29, local copies, waits for them, and re-layouts  9.88 us

commit v1 on v0

--- a/solution.py
+++ b/solution.py
@@ -53,23 +53,26 @@
     return tz * 16 + tx * 4 + ty, tc
 
 
-def mixer(carried, mask, gains, weights):
-    groups, rows, width = carried.shape
+def mixer(flat, mask, gains, weights):
+    width = flat.shape[1]
+    pieces = [slice(g * 128, g * 128 + 128) for g in range(flat.shape[0] // 128)]
     query, key, value, out, up, down = weights
-    flat = carried.reshape(groups * rows, width)
     normed = rms(flat, gains[0]).astype(BF16)
-    queries = dot(normed, query).astype(BF16)
-    keys = dot(normed, key).astype(BF16)
-    values = dot(normed, value).astype(BF16)
-    pieces = []
-    for g in range(groups):
-        part = slice(g * rows, (g + 1) * rows)
-        scores = dot_nt(queries[part], keys[part]) * (width**-0.5)
-        scores = jnp.where(mask, scores, -1e30)
-        exponent = jnp.exp(scores - jnp.max(scores, axis=-1, keepdims=True))
-        attention = exponent * (1.0 / jnp.sum(exponent, axis=-1, keepdims=True))
-        pieces.append(dot(attention.astype(BF16), values[part]).astype(BF16))
-    attended = jnp.concatenate(pieces, axis=0) if groups > 1 else pieces[0]
+    projected = dot(normed, jnp.concatenate([query, key, value], axis=1)).astype(BF16)
+    queries = projected[:, :width]
+    keys = projected[:, width : 2 * width]
+    values = projected[:, 2 * width :]
+    ones = jnp.ones((128, width), BF16)
+    scores = [
+        jnp.where(mask, dot_nt(queries[p], keys[p]), -1e30) * (width**-0.5) for p in pieces
+    ]
+    exponent = [jnp.exp(s - jnp.max(s, axis=-1, keepdims=True)).astype(BF16) for s in scores]
+    summed = [
+        dot(e, jnp.concatenate([values[p], ones], axis=1)) for e, p in zip(exponent, pieces)
+    ]
+    attended = jnp.concatenate(
+        [(s[:, :width] * (1.0 / s[:, width:])).astype(BF16) for s in summed], axis=0
+    )
     residual = flat + dot(attended, out)
     again = rms(residual, gains[1]).astype(BF16)
     hidden = gelu(dot(again, up)).astype(BF16)
@@ -268,24 +271,27 @@
         paired = pool[x, pl.ds(0, 128, stride=2), :] + pool[x, pl.ds(1, 128, stride=2), :]
         filt[:, x, :] = dot_nt(pick, paired, HIGHEST)
 
+    slot = (gx // 4) * 8 + gy * 4 + lax.rem(gx, 4)
+
     def send_filtered(step, carry):
         tx, ty = peer(step, gx, gy)
         pltpu.make_async_remote_copy(
-            src_ref=filt.at[tx * 2 + ty], dst_ref=recv.at[gy * 32 + gx], send_sem=a_send,
+            src_ref=filt.at[tx * 2 + ty], dst_ref=recv.at[slot], send_sem=a_send,
             recv_sem=a_recv, device_id={"gx": tx, "gy": ty}, device_id_type=MESH,
         ).start()
         return carry
 
     lax.fori_loop(0, 63, send_filtered, 0)
-    recv[pl.ds(gy * 32 + gx, 1)] = filt[pl.ds(plane, 1)]
+    recv[pl.ds(slot, 1)] = filt[pl.ds(plane, 1)]
 
     for copy in weight_loads:
         copy.wait()
     lift_rows = jnp.concatenate(
         [jnp.broadcast_to(lift_w[c : c + 1, :], (16, 128)) for c in range(8)], axis=0
     )
-    head_lanes = jnp.concatenate(
-        [jnp.broadcast_to(head_w[:, f : f + 1].astype(F32), (128, 32)) for f in range(4)], axis=1
+    head_all = head_w[...].astype(F32)
+    head_rows = jnp.concatenate(
+        [jnp.broadcast_to(head_all[f : f + 1, :], (32, 128)) for f in range(4)], axis=0
     ).astype(BF16)
 
     a_all = pltpu.make_async_remote_copy(
@@ -295,7 +301,6 @@
     a_all.wait_recv()
 
     filtered = jnp.concatenate([recv[:, 0, :], recv[:, 1, :]], axis=0)
-    along_x = lax.rem(rows // 32, 2) == lax.rem(lanes // 32, 2)
     lane16 = lax.rem(lanes, 16)
 
     def block_weights(i):
@@ -304,41 +309,34 @@
     def gain(i):
         return gains_w[i : i + 1, :]
 
-    GROUP = 4
-
-    def x_block(step, carry):
-        inputs = jnp.concatenate(
-            [jnp.where(lane16 == step * GROUP + g, filtered, 0.0) for g in range(GROUP)], axis=0
-        )
-        lifted = (
-            jnp.dot(inputs, lift_rows, precision=HIGHEST, preferred_element_type=F32) + bias_w[...]
-        )
-        features = gelu(rms(lifted, gain(0))).astype(BF16).astype(F32)
-        result = mixer(
-            features.reshape(GROUP, 128, 128), along_x, (gain(1), gain(2)), block_weights(0)
-        )
-        hid[pl.ds(step * GROUP, GROUP)] = result.astype(F32).reshape(GROUP, 2, 2, 32, 128)
-        return carry
-
-    lax.fori_loop(0, 16 // GROUP, x_block, 0)
-
-    along_y = lax.rem(iota((256, 256), 0), 8) == lax.rem(iota((256, 256), 1), 8)
-    cell = iota((32, 8, 128), 0)
-    own_lane = lax.rem(iota((32, 8, 128), 2), 32) == lax.rem(cell, 2) * 16 + cell // 2
-
-    def y_block(x, g):
-        lines = hid[:, x, :, 8 * g : 8 * g + 8, :].reshape(1, 256, 128)
-        result = mixer(lines, along_y, (gain(3), gain(4)), block_weights(1))
-        final = rms(result.astype(F32), gain(5)).astype(BF16)
-        spread = dot(final, head_lanes).reshape(32, 8, 128)
-        logits = jnp.sum(jnp.where(own_lane, spread, 0.0), axis=0)
+    inputs = jnp.concatenate(
+        [jnp.where(lane16 == y, filtered, 0.0) for y in range(16)], axis=0
+    )
+    lifted = (
+        jnp.dot(inputs, lift_rows, precision=HIGHEST, preferred_element_type=F32) + bias_w[...]
+    )
+    features = gelu(rms(lifted, gain(0))).astype(BF16).astype(F32)
+    along_x = lax.rem(rows // 4, 2) == lax.rem(lanes // 4, 2)
+    result = mixer(features, along_x, (gain(1), gain(2)), block_weights(0))
+    for y in range(16):
+        part = result[y * 128 : y * 128 + 128].astype(F32)
+        for c in range(16):
+            hid[c, y] = part[c * 8 : c * 8 + 8]
+
+    along_y = lax.rem(rows, 4) == lax.rem(lanes, 4)
+    result = mixer(
+        hid[...].reshape(2048, 128), along_y, (gain(3), gain(4)), block_weights(1)
+    )
+    final = rms(result.astype(F32), gain(5)).astype(BF16)
+    spread = dot_nt(final, head_rows)
+    own_lane = lax.rem(lanes, 32) == lax.rem(rows // 4, 2) * 16 + rows // 8
+    for c in range(16):
+        part = jnp.where(own_lane, spread[c * 128 : c * 128 + 128], 0.0).reshape(16, 8, 128)
+        part = jnp.sum(part, axis=0)
+        logits = part + pltpu.roll(part, 4, 0)
         coefficient = 0.05 + 0.45 * (1.0 / (1.0 + jnp.exp(-logits)))
-        for r in range(8):
-            cbuf[1 + x + 2 * (8 * g + r)] = coefficient[r : r + 1, :]
-
-    for x in range(2):
-        for g in range(4):
-            y_block(x, g)
+        for r in range(4):
+            cbuf[1 + c // 8 + 2 * (4 * (c % 8) + r)] = coefficient[r : r + 1, :]
     cbuf[0] = cbuf[64]
     cbuf[65] = cbuf[1]
 
@@ -394,9 +392,11 @@
     final_copy.wait()
 
 
-def refine_kernel(next_in, coarse, next_out, eddy, sem):
-    copy = pltpu.make_async_copy(next_in, next_out, sem)
-    copy.start()
+def refine_kernel(next_hbm, coarse_hbm, next_out, eddy_hbm, coarse, passed, eddy, sem):
+    load = pltpu.make_async_copy(coarse_hbm, coarse, sem.at[0])
+    load.start()
+    first = pltpu.make_async_copy(next_hbm, passed, sem.at[1])
+    first.start()
     gy = lax.axis_index("gy")
     row, column = iota((128, 128), 0), iota((128, 128), 1)
     fine = lax.rem(column, 32)
@@ -410,7 +410,9 @@
     centre = 1 + column // 2
     other = centre - 1 + 2 * lax.rem(column, 2)
     along_z = jnp.where(row == centre, 0.75, 0.0) + jnp.where(row == other, 0.25, 0.0)
+    load.wait()
     cells = [coarse[:, x, 0, :] for x in range(4)]
+    results = []
     for x in range(4):
         centre, other = (1, 0, 1, 2, 2, 1, 2, 3)[2 * x : 2 * x + 2]
         mixed = 0.75 * cells[centre] + 0.25 * cells[other]
@@ -418,15 +420,22 @@
         full = lax.dot_general(
             wide, along_z, (((0,), (0,)), ((), ())), precision=HIGHEST, preferred_element_type=F32
         )
-        eddy[:, x] = full.reshape(4, 32, 128)
-    copy.wait()
+        eddy[x] = full.reshape(4, 32, 128)
+        results.append(pltpu.make_async_copy(eddy.at[x], eddy_hbm.at[:, x], sem.at[3 + x]))
+        results[-1].start()
+        if x == 0:
+            first.wait()
+            results.append(pltpu.make_async_copy(passed, next_out, sem.at[2]))
+            results[-1].start()
+    for copy in results:
+        copy.wait()
 
 
 def per_device(state, visc, lift, bias, gains, query, key, value, out, up, down, head):
     hbm = pl.BlockSpec(memory_space=pl.ANY)
     vmem = pltpu.VMEM
     block = (4, 4, 32, 128)
-    weights = (lift, bias.reshape(1, 128), gains, query, key, value, out, up, down, head)
+    weights = (lift, bias.reshape(1, 128), gains, query, key, value, out, up, down, head.T)
     state_next, coarse = pl.pallas_call(
         main_kernel,
         out_shape=(
@@ -449,7 +458,7 @@
             vmem((2, 256, 128), F32),
             vmem((64, 2, 128), F32),
             vmem((64, 2, 128), F32),
-            vmem((16, 2, 2, 32, 128), F32),
+            vmem((16, 16, 8, 128), F32),
             vmem((66, 1, 128), F32),
             vmem((72, 4, 1, 128), F32),
         ]
@@ -467,16 +476,22 @@
             DMA((5,)),
         ],
         compiler_params=pltpu.CompilerParams(
-            collective_id=0, has_side_effects=True, vmem_limit_bytes=48 << 20
+            collective_id=0, has_side_effects=True, vmem_limit_bytes=60 << 20
         ),
         name="flow_and_columns",
     )(state, visc, *weights)
     return pl.pallas_call(
         refine_kernel,
         out_shape=(jax.ShapeDtypeStruct(block, F32), jax.ShapeDtypeStruct(block, F32)),
-        in_specs=[hbm, pl.BlockSpec(memory_space=pltpu.VMEM)],
-        out_specs=(hbm, pl.BlockSpec(memory_space=pltpu.VMEM)),
-        scratch_shapes=[DMA],
+        in_specs=[hbm, hbm],
+        out_specs=(hbm, hbm),
+        scratch_shapes=[
+            vmem((72, 4, 1, 128), F32),
+            vmem(block, F32),
+            vmem(block, F32),
+            DMA((7,)),
+        ],
+        compiler_params=pltpu.CompilerParams(vmem_limit_bytes=60 << 20),
         name="refine",
     )(state_next, coarse)
 

time: 104 us -> 73.1 us (0.70)
  Pallas kernels: 92.6 us -> 72.4 us
  local copies, waits for them, and re-layouts: 9.88 us -> 0 us
    pallas_call x1, Pallas kernels: 81.9 us -> 69.1 us  [per_device(): pl.pallas_call(main_kernel, out_shape=(jax.ShapeDtypeStruct(block, F32),...]
    unnamed x29 -> x0, local copies, waits for them, and re-layouts: 9.88 us -> none
    pallas_call x1, Pallas kernels: 10.7 us -> 3.28 us  [per_device(): pl.pallas_call(refine_kernel, out_shape=(jax.ShapeDtypeStruct(block, F32)...]
where the time goes in v1:
time: 73.1 us; the launch traced here: 73 us
  Pallas kernels  72.4 us (99%)
    pallas_call x1, Pallas kernels, per_device(): pl.pallas_call(main_kernel, out_shape=(jax.ShapeDtypeStruct(block, F32),...  69.1 us
    pallas_call x1, Pallas kernels, per_device(): pl.pallas_call(refine_kernel, out_shape=(jax.ShapeDtypeStruct(block, F32)...  3.28 us

profile of v1, /device:TPU:1, one launch (start us, length us, event | category | flops | bytes accessed | tf_op | source)
XLA Modules:
  0.0 73.0 jit_solution(6870373269166908581)
XLA Ops:
  0.6 69.1 %flow_and_columns.1 = (f32[4,4,32,128]{3,2,1,0:T(8,128)}, f32[72,4,1,128]{3,2,1,0:T(1,128)}) custom-call(f32[4,4,32,128]{3,2,1,0:T(8,128)} %state_hbm.1, f32[4,4,32,128]{3,2,1,0:T(8,128)} %visc_hbm.1, f32[8,128]{1,0:T(8,128)} %lift_hbm.1, f32[1,128]{1,0:T(1,128)} %bitcast.3, f32[6,128]{1,0:T(8,128)} %gains_hbm.1, bf16[2,128,128]{2,1,0:T(8,128)(2,1)} %query_hbm.1, ...), custom_call_target="tpu_custom_call" | custom-call | tf_op jit(solution)/shard_map/flow_and_columns/pallas_call | solution.py:439
  69.7 3.3 %refine.1 = (f32[4,4,32,128]{3,2,1,0:T(8,128)}, f32[4,4,32,128]{3,2,1,0:T(8,128)}) custom-call(f32[4,4,32,128]{3,2,1,0:T(8,128)} %get-tuple-element.4.next_hbm, f32[72,4,1,128]{3,2,1,0:T(1,128)} %get-tuple-element.5.coarse_hbm), custom_call_target="tpu_custom_call" | custom-call | tf_op jit(solution)/shard_map/refine/pallas_call | solution.py:483

commit v2 on v1

--- a/solution.py
+++ b/solution.py
@@ -1,4 +1,3 @@
-import functools
 import math
 
 import jax
@@ -41,16 +40,20 @@
     )
 
 
-def order4(step):
-    return lax.rem(2 + 3 * step + 3 * (step // 2) + 2 * (step // 3), 4)
-
-
-def peer(step, gx, gy):
-    tz = lax.rem(gx // 16 + 1 + step // 32, 2)
-    tx = lax.rem(lax.rem(gx // 4, 4) + order4(lax.rem(step // 8, 4)), 4)
-    ty = lax.rem(lax.rem(gx, 4) + order4(lax.rem(step // 2, 4)), 4)
-    tc = lax.rem(gy + 1 + lax.rem(step, 2), 2)
-    return tz * 16 + tx * 4 + ty, tc
+def peers(gx, gy):
+    z, x, y = gx // 16, lax.rem(gx // 4, 4), lax.rem(gx, 4)
+
+    def ring(place):
+        return [lax.rem(place + 2, 4), lax.rem(place + 1, 4), lax.rem(place + 3, 4), place]
+
+    found = [
+        (tz * 16 + tx * 4 + ty, tc)
+        for tz in (1 - z, z)
+        for tx in ring(x)
+        for ty in ring(y)
+        for tc in (1 - gy, gy)
+    ]
+    return found[:63]
 
 
 def mixer(flat, mask, gains, weights):
@@ -82,18 +85,32 @@
 def main_kernel(
     state_hbm, visc_hbm, lift_hbm, bias_hbm, gains_hbm, query_hbm, key_hbm, value_hbm, out_hbm,
     up_hbm, down_hbm, head_hbm,
-    next_hbm, coarse_hbm,
-    s0, s1, s2, s3, visc, nu_f, nu_b, nu_sum, xs, xr, ys, yr, zs, zr, pool, filt, recv, hid, cbuf,
+    s3, eddy,
+    s0, s1, s2, visc, nu_f, nu_b, nu_sum, xs, xr, ys, yr, zs, zr, pool, filt, recv, hid, cbuf,
     ebuf, lift_w, bias_w, gains_w, query_w, key_w, value_w, out_w, up_w, down_w, head_w,
-    load_sem, weight_sem, face_send, face_recv, a_send, a_recv, b_send, b_recv, edge_send, out_sem,
+    load_sem, weight_sem, face_send, face_recv, a_send, a_recv, b_send, b_recv, edge_send,
 ):
     gx, gy, gz = lax.axis_index("gx"), lax.axis_index("gy"), lax.axis_index("gz")
     plane = gx * 2 + gy
+    others = peers(gx, gy)
     loads = []
-    for x in range(4):
+    for x in (0, 3, 1, 2):
         for n, (src, dst) in enumerate(((state_hbm, s0), (visc_hbm, visc))):
             loads.append(pltpu.make_async_copy(src.at[:, x], dst.at[x], load_sem.at[n, x]))
             loads[-1].start()
+
+    barrier = pltpu.get_barrier_semaphore()
+    z_next, z_last = lax.rem(gz + 1, 4), lax.rem(gz + 3, 4)
+    for tx, ty in others:
+        pl.semaphore_signal(barrier, inc=1, device_id={"gx": tx, "gy": ty}, device_id_type=MESH)
+    for target in (z_next, z_last):
+        pl.semaphore_signal(barrier, inc=1, device_id={"gz": target}, device_id_type=MESH)
+    pl.semaphore_signal(
+        barrier, inc=1, device_id={"gx": 0, "gy": 0, "gz": z_next}, device_id_type=MESH
+    )
+    pl.semaphore_signal(
+        barrier, inc=1, device_id={"gx": 31, "gy": 1, "gz": z_last}, device_id_type=MESH
+    )
     weight_pairs = (
         (lift_hbm, lift_w), (bias_hbm, bias_w), (gains_hbm, gains_w), (query_hbm, query_w),
         (key_hbm, key_w), (value_hbm, value_w), (out_hbm, out_w), (up_hbm, up_w),
@@ -104,32 +121,16 @@
         weight_loads.append(pltpu.make_async_copy(src, dst, weight_sem.at[n]))
         weight_loads[-1].start()
 
-    barrier = pltpu.get_barrier_semaphore()
-
-    def greet(step, carry):
-        tx, ty = peer(step, gx, gy)
-        pl.semaphore_signal(barrier, inc=1, device_id={"gx": tx, "gy": ty}, device_id_type=MESH)
-        return carry
-
-    z_next, z_last = lax.rem(gz + 1, 4), lax.rem(gz + 3, 4)
-    lax.fori_loop(0, 63, greet, 0)
-    for target in (z_next, z_last):
-        pl.semaphore_signal(barrier, inc=1, device_id={"gz": target}, device_id_type=MESH)
-    pl.semaphore_signal(
-        barrier, inc=1, device_id={"gx": 0, "gy": 0, "gz": z_next}, device_id_type=MESH
-    )
-    pl.semaphore_signal(
-        barrier, inc=1, device_id={"gx": 31, "gy": 1, "gz": z_last}, device_id_type=MESH
-    )
-
     for copy in loads:
         copy.wait()
 
     lanes32 = iota((32, 128), 1)
 
-    def stage(e, source):
+    def stage_x(e, source):
         xs[e, 0] = source[0].astype(BF16)
         xs[e, 1] = source[3].astype(BF16)
+
+    def stage_yz(e, source):
         packed = jnp.zeros((32, 128), F32)
         for x in range(4):
             for f in range(4):
@@ -159,14 +160,33 @@
             for n, (src, dst, device) in enumerate(pairs)
         ]
 
-    stage(0, s0)
-    stage(1, visc)
+    copies = [face_copies(e) for e in range(4)]
+
+    def start_x(e):
+        copies[e][0].start()
+        copies[e][1].start()
+
+    def start_yz(e):
+        for copy in copies[e][2:]:
+            copy.start()
+
+    def wait_x(e):
+        copies[e][0].wait_recv()
+        copies[e][1].wait_recv()
+
+    def wait_yz(e):
+        for copy in copies[e][2:]:
+            copy.wait_recv()
+
+    stage_x(1, visc)
+    stage_x(0, s0)
     extra = jnp.where(plane == 0, 64, 0) + jnp.where(plane == 63, 64, 0)
     pl.semaphore_wait(barrier, 65 + extra)
-    copies = [face_copies(e) for e in range(4)]
-    for e in range(2):
-        for copy in copies[e]:
-            copy.start()
+    for e, source in ((1, visc), (0, s0)):
+        start_x(e)
+    for e, source in ((1, visc), (0, s0)):
+        stage_yz(e, source)
+        start_yz(e)
 
     rows = iota((128, 128), 0)
     lanes = iota((128, 128), 1)
@@ -210,8 +230,8 @@
         z_f = jnp.where(lanes == 127, column(1, 0), pltpu.roll(middle, 127, 1))
         return middle, ((x_b, x_f), (y_b, y_f), (z_b, z_f))
 
-    def advance(e, source, combine):
-        for x in range(4):
+    def advance(e, source, combine, planes):
+        for x in planes:
             middle, pairs = neighbours(e, source, x)
             total = -middle * nu_sum[x]
             for d, (before, after) in enumerate(pairs):
@@ -220,18 +240,17 @@
                 total += after * (nu_f[d, x] - half) + before * (nu_b[d, x] + half)
             combine(x, middle + total)
 
-    for copy in copies[1]:
-        copy.wait_recv()
-    for x in range(4):
-        middle, pairs = neighbours(1, visc, x)
-        total = jnp.zeros((128, 128), F32)
-        for d, (before, after) in enumerate(pairs):
-            forward = (0.5 * TIME_STEP) * (middle + after)
-            backward = (0.5 * TIME_STEP) * (middle + before)
-            nu_f[d, x] = forward
-            nu_b[d, x] = backward
-            total += forward + backward
-        nu_sum[x] = total
+    def mean_viscosity(planes):
+        for x in planes:
+            middle, pairs = neighbours(1, visc, x)
+            total = jnp.zeros((128, 128), F32)
+            for d, (before, after) in enumerate(pairs):
+                forward = (0.5 * TIME_STEP) * (middle + after)
+                backward = (0.5 * TIME_STEP) * (middle + before)
+                nu_f[d, x] = forward
+                nu_b[d, x] = backward
+                total += forward + backward
+            nu_sum[x] = total
 
     def first(x, value):
         s1[x] = value.reshape(4, 32, 128)
@@ -240,32 +259,29 @@
         s2[x] = (0.75 * s0[x].reshape(128, 128) + 0.25 * value).reshape(4, 32, 128)
 
     def third(x, value):
-        s3[x] = (s0[x].reshape(128, 128) / 3.0 + (2.0 / 3.0) * value).reshape(4, 32, 128)
-
-    for copy in copies[0]:
-        copy.wait_recv()
-    advance(0, s0, first)
-    stage(2, s1)
-    for copy in copies[2]:
-        copy.start()
-    for copy in copies[2]:
-        copy.wait_recv()
-    advance(2, s1, second)
-    stage(3, s2)
-    for copy in copies[3]:
-        copy.start()
-    for copy in copies[3]:
-        copy.wait_recv()
-    advance(3, s2, third)
-
-    results = []
-    for x in range(4):
-        results.append(pltpu.make_async_copy(s3.at[x], next_hbm.at[:, x], out_sem.at[x]))
-        results[-1].start()
+        s3[:, x] = (s0[x].reshape(128, 128) / 3.0 + (2.0 / 3.0) * value).reshape(4, 32, 128)
+
+    wait_yz(1)
+    mean_viscosity((1, 2))
+    wait_yz(0)
+    advance(0, s0, first, (1, 2))
+    wait_x(1)
+    mean_viscosity((0, 3))
+    wait_x(0)
+    advance(0, s0, first, (0, 3))
+    for e, source, target, combine in ((2, s1, s2, second), (3, s2, s3, third)):
+        stage_x(e, source)
+        start_x(e)
+        stage_yz(e, source)
+        start_yz(e)
+        wait_yz(e)
+        advance(e, source, combine, (1, 2))
+        wait_x(e)
+        advance(e, source, combine, (0, 3))
 
     pick = jnp.where(iota((64, 128), 1) // 2 == iota((64, 128), 0), 0.125, 0.0)
     for x in range(2):
-        one, two = s3[2 * x].reshape(128, 128), s3[2 * x + 1].reshape(128, 128)
+        one, two = (s3[:, 2 * x + i].reshape(128, 128) for i in range(2))
         pool[x, 0:128] = one + two
         pool[x, 128:256] = one * one + two * two
         paired = pool[x, pl.ds(0, 128, stride=2), :] + pool[x, pl.ds(1, 128, stride=2), :]
@@ -273,15 +289,11 @@
 
     slot = (gx // 4) * 8 + gy * 4 + lax.rem(gx, 4)
 
-    def send_filtered(step, carry):
-        tx, ty = peer(step, gx, gy)
+    for tx, ty in others:
         pltpu.make_async_remote_copy(
             src_ref=filt.at[tx * 2 + ty], dst_ref=recv.at[slot], send_sem=a_send,
             recv_sem=a_recv, device_id={"gx": tx, "gy": ty}, device_id_type=MESH,
         ).start()
-        return carry
-
-    lax.fori_loop(0, 63, send_filtered, 0)
     recv[pl.ds(slot, 1)] = filt[pl.ds(plane, 1)]
 
     for copy in weight_loads:
@@ -340,65 +352,36 @@
     cbuf[0] = cbuf[64]
     cbuf[65] = cbuf[1]
 
-    def send_coarse(step, carry):
-        tx, ty = peer(step, gx, gy)
-        pltpu.make_async_remote_copy(
-            src_ref=cbuf.at[pl.ds(2 * tx, 4)], dst_ref=ebuf.at[plane + 1], send_sem=b_send,
-            recv_sem=b_recv, device_id={"gx": tx, "gy": ty}, device_id_type=MESH,
-        ).start()
-        return carry
-
-    def send_edge(slot, target_z, step, carry):
-        tx, ty = peer(step, gx, gy)
-        pltpu.make_async_remote_copy(
-            src_ref=cbuf.at[pl.ds(2 * tx, 4)], dst_ref=ebuf.at[slot], send_sem=edge_send,
-            recv_sem=b_recv, device_id={"gx": tx, "gy": ty, "gz": target_z}, device_id_type=MESH,
-        ).start()
-        return carry
-
-    @pl.when(plane == 63)
-    def _():
-        lax.fori_loop(0, 64, functools.partial(send_edge, 0, z_next), 0)
-
-    @pl.when(plane == 0)
-    def _():
-        lax.fori_loop(0, 64, functools.partial(send_edge, 65, z_last), 0)
-
-    lax.fori_loop(0, 63, send_coarse, 0)
+    def send_edge(slot, target_z, targets):
+        for tx, ty in targets:
+            pltpu.make_async_remote_copy(
+                src_ref=cbuf.at[pl.ds(2 * tx, 4)], dst_ref=ebuf.at[slot], send_sem=edge_send,
+                recv_sem=b_recv, device_id={"gx": tx, "gy": ty, "gz": target_z},
+                device_id_type=MESH,
+            ).start()
+
+    for half in (slice(0, 32), slice(32, 64)):
+        for tx, ty in others[half]:
+            pltpu.make_async_remote_copy(
+                src_ref=cbuf.at[pl.ds(2 * tx, 4)], dst_ref=ebuf.at[plane + 1], send_sem=b_send,
+                recv_sem=b_recv, device_id={"gx": tx, "gy": ty}, device_id_type=MESH,
+            ).start()
+
+        @pl.when(plane == 63)
+        def _(half=half):
+            send_edge(0, z_next, (others + [(gx, gy)])[half])
+
+        @pl.when(plane == 0)
+        def _(half=half):
+            send_edge(65, z_last, (others + [(gx, gy)])[half])
+
     ebuf[pl.ds(plane + 1, 1)] = cbuf[pl.ds(2 * gx, 4)].reshape(1, 4, 1, 128)
     ebuf[66:72] = jnp.zeros((6, 4, 1, 128), F32)
     b_all = pltpu.make_async_remote_copy(
         src_ref=ebuf.at[pl.ds(0, 63)], dst_ref=ebuf.at[pl.ds(0, 65)], send_sem=b_send,
         recv_sem=b_recv, device_id={"gy": 1 - gy}, device_id_type=MESH,
     )
-    b_all.wait_recv()
-    final_copy = pltpu.make_async_copy(ebuf, coarse_hbm, out_sem.at[4])
-    final_copy.start()
-    for e in range(4):
-        for copy in copies[e]:
-            copy.wait_send()
-    a_all.wait_send()
-    b_all.wait_send()
-
-    @pl.when((plane == 63) | (plane == 0))
-    def _():
-        pltpu.make_async_remote_copy(
-            src_ref=ebuf.at[pl.ds(0, 64)], dst_ref=ebuf.at[pl.ds(0, 64)], send_sem=edge_send,
-            recv_sem=b_recv, device_id={"gy": 1 - gy}, device_id_type=MESH,
-        ).wait_send()
-
-    for copy in results:
-        copy.wait()
-    final_copy.wait()
-
-
-def refine_kernel(next_hbm, coarse_hbm, next_out, eddy_hbm, coarse, passed, eddy, sem):
-    load = pltpu.make_async_copy(coarse_hbm, coarse, sem.at[0])
-    load.start()
-    first = pltpu.make_async_copy(next_hbm, passed, sem.at[1])
-    first.start()
-    gy = lax.axis_index("gy")
-    row, column = iota((128, 128), 0), iota((128, 128), 1)
+    row, column = rows, lanes
     fine = lax.rem(column, 32)
     centre = gy * 16 + fine // 2
     other = lax.rem(centre + 31 + 2 * lax.rem(fine, 2), 32)
@@ -410,9 +393,8 @@
     centre = 1 + column // 2
     other = centre - 1 + 2 * lax.rem(column, 2)
     along_z = jnp.where(row == centre, 0.75, 0.0) + jnp.where(row == other, 0.25, 0.0)
-    load.wait()
-    cells = [coarse[:, x, 0, :] for x in range(4)]
-    results = []
+    b_all.wait_recv()
+    cells = [ebuf[:, x, 0, :] for x in range(4)]
     for x in range(4):
         centre, other = (1, 0, 1, 2, 2, 1, 2, 3)[2 * x : 2 * x + 2]
         mixed = 0.75 * cells[centre] + 0.25 * cells[other]
@@ -420,14 +402,29 @@
         full = lax.dot_general(
             wide, along_z, (((0,), (0,)), ((), ())), precision=HIGHEST, preferred_element_type=F32
         )
-        eddy[x] = full.reshape(4, 32, 128)
-        results.append(pltpu.make_async_copy(eddy.at[x], eddy_hbm.at[:, x], sem.at[3 + x]))
-        results[-1].start()
-        if x == 0:
-            first.wait()
-            results.append(pltpu.make_async_copy(passed, next_out, sem.at[2]))
-            results[-1].start()
-    for copy in results:
+        eddy[:, x] = full.reshape(4, 32, 128)
+    for e in range(4):
+        for copy in copies[e]:
+            copy.wait_send()
+    a_all.wait_send()
+    b_all.wait_send()
+
+    @pl.when((plane == 63) | (plane == 0))
+    def _():
+        pltpu.make_async_remote_copy(
+            src_ref=ebuf.at[pl.ds(0, 64)], dst_ref=ebuf.at[pl.ds(0, 64)], send_sem=edge_send,
+            recv_sem=b_recv, device_id={"gy": 1 - gy}, device_id_type=MESH,
+        ).wait_send()
+
+
+def store_kernel(first, second, first_out, second_out, sem):
+    copies = [
+        pltpu.make_async_copy(first, first_out, sem.at[0]),
+        pltpu.make_async_copy(second, second_out, sem.at[1]),
+    ]
+    for copy in copies:
+        copy.start()
+    for copy in copies:
         copy.wait()
 
 
@@ -436,15 +433,12 @@
     vmem = pltpu.VMEM
     block = (4, 4, 32, 128)
     weights = (lift, bias.reshape(1, 128), gains, query, key, value, out, up, down, head.T)
-    state_next, coarse = pl.pallas_call(
+    results = pl.pallas_call(
         main_kernel,
-        out_shape=(
-            jax.ShapeDtypeStruct(block, F32),
-            jax.ShapeDtypeStruct((72, 4, 1, 128), F32),
-        ),
+        out_shape=(vmem(block, F32), vmem(block, F32)),
         in_specs=[hbm] * 12,
-        out_specs=(hbm, hbm),
-        scratch_shapes=[vmem(block, F32)] * 5
+        out_specs=(pl.BlockSpec(memory_space=vmem),) * 2,
+        scratch_shapes=[vmem(block, F32)] * 4
         + [
             vmem((3, 4, 128, 128), F32),
             vmem((3, 4, 128, 128), F32),
@@ -473,7 +467,6 @@
             DMA,
             DMA,
             DMA,
-            DMA((5,)),
         ],
         compiler_params=pltpu.CompilerParams(
             collective_id=0, has_side_effects=True, vmem_limit_bytes=60 << 20
@@ -481,19 +474,14 @@
         name="flow_and_columns",
     )(state, visc, *weights)
     return pl.pallas_call(
-        refine_kernel,
-        out_shape=(jax.ShapeDtypeStruct(block, F32), jax.ShapeDtypeStruct(block, F32)),
+        store_kernel,
+        out_shape=(jax.ShapeDtypeStruct(block, F32),) * 2,
         in_specs=[hbm, hbm],
         out_specs=(hbm, hbm),
-        scratch_shapes=[
-            vmem((72, 4, 1, 128), F32),
-            vmem(block, F32),
-            vmem(block, F32),
-            DMA((7,)),
-        ],
-        compiler_params=pltpu.CompilerParams(vmem_limit_bytes=60 << 20),
-        name="refine",
-    )(state_next, coarse)
+        scratch_shapes=[DMA((2,))],
+        compiler_params=pltpu.CompilerParams(vmem_limit_bytes=1 << 20),
+        name="store",
+    )(*results)
 
 
 def solution(mesh):

time: 73.1 us -> 63.2 us (0.86)
  Pallas kernels: 72.4 us -> 62.2 us
    pallas_call x2, Pallas kernels: 72.4 us -> 62.2 us  [the longest x1 61.4 us: per_device(): pl.pallas_call(main_kernel, out_shape=(vmem(block, F32), vmem(block, F32)...]
where the time goes in v2:
time: 63.2 us; the launch traced here: 63.1 us
  Pallas kernels  62.2 us (98%)
  between operations  0.8 us (1%)
    pallas_call x1, Pallas kernels, per_device(): pl.pallas_call(main_kernel, out_shape=(vmem(block, F32), vmem(block, F32)...  61.4 us

profile of v2, /device:TPU:1, one launch (start us, length us, event | category | flops | bytes accessed | tf_op | source)
XLA Modules:
  0.0 63.1 jit_solution(16288196687452424875)
XLA Ops:
  0.6 61.4 %flow_and_columns.1 = (f32[4,4,32,128]{3,2,1,0:T(8,128)S(1)}, f32[4,4,32,128]{3,2,1,0:T(8,128)S(1)}) custom-call(f32[4,4,32,128]{3,2,1,0:T(8,128)} %state_hbm.1, f32[4,4,32,128]{3,2,1,0:T(8,128)} %visc_hbm.1, f32[8,128]{1,0:T(8,128)} %lift_hbm.1, f32[1,128]{1,0:T(1,128)} %bitcast.3, f32[6,128]{1,0:T(8,128)} %gains_hbm.1, bf16[2,128,128]{2,1,0:T(8,128)(2,1)} %query_hbm.1, ...), custom_call_target="tpu_custom_call" | custom-call | tf_op jit(solution)/shard_map/flow_and_columns/pallas_call | solution.py:436
  62.1 0.8 %store.1 = (f32[4,4,32,128]{3,2,1,0:T(8,128)}, f32[4,4,32,128]{3,2,1,0:T(8,128)}) custom-call(f32[4,4,32,128]{3,2,1,0:T(8,128)S(1)} %get-tuple-element.4.first, f32[4,4,32,128]{3,2,1,0:T(8,128)S(1)} %get-tuple-element.5.second), custom_call_target="tpu_custom_call" | custom-call | tf_op jit(solution)/shard_map/store/pallas_call | solution.py:476

commit v3 on v2

--- a/solution.py
+++ b/solution.py
@@ -18,6 +18,14 @@
 
 def iota(shape, dim):
     return lax.broadcasted_iota(jnp.int32, shape, dim)
+
+
+def split(values, count):
+    parts = []
+    for _ in range(count):
+        parts.append(values.astype(BF16))
+        values = values - parts[-1].astype(F32)
+    return parts
 
 
 def rms(values, gain):
@@ -56,12 +64,16 @@
     return found[:63]
 
 
-def mixer(flat, mask, gains, weights):
+def project(flat, gain, weights):
+    query, key, value = weights[:3]
+    normed = rms(flat, gain).astype(BF16)
+    return dot(normed, jnp.concatenate([query, key, value], axis=1)).astype(BF16)
+
+
+def mixer(flat, projected, mask, gain, weights):
     width = flat.shape[1]
     pieces = [slice(g * 128, g * 128 + 128) for g in range(flat.shape[0] // 128)]
-    query, key, value, out, up, down = weights
-    normed = rms(flat, gains[0]).astype(BF16)
-    projected = dot(normed, jnp.concatenate([query, key, value], axis=1)).astype(BF16)
+    out, up, down = weights[3:]
     queries = projected[:, :width]
     keys = projected[:, width : 2 * width]
     values = projected[:, 2 * width :]
@@ -77,7 +89,7 @@
         [(s[:, :width] * (1.0 / s[:, width:])).astype(BF16) for s in summed], axis=0
     )
     residual = flat + dot(attended, out)
-    again = rms(residual, gains[1]).astype(BF16)
+    again = rms(residual, gain).astype(BF16)
     hidden = gelu(dot(again, up)).astype(BF16)
     return (residual + dot(hidden, down)).astype(BF16)
 
@@ -111,17 +123,7 @@
     pl.semaphore_signal(
         barrier, inc=1, device_id={"gx": 31, "gy": 1, "gz": z_last}, device_id_type=MESH
     )
-    weight_pairs = (
-        (lift_hbm, lift_w), (bias_hbm, bias_w), (gains_hbm, gains_w), (query_hbm, query_w),
-        (key_hbm, key_w), (value_hbm, value_w), (out_hbm, out_w), (up_hbm, up_w),
-        (down_hbm, down_w), (head_hbm, head_w),
-    )
-    weight_loads = []
-    for n, (src, dst) in enumerate(weight_pairs):
-        weight_loads.append(pltpu.make_async_copy(src, dst, weight_sem.at[n]))
-        weight_loads[-1].start()
-
-    for copy in loads:
+    for copy in loads[:4]:
         copy.wait()
 
     lanes32 = iota((32, 128), 1)
@@ -184,9 +186,21 @@
     pl.semaphore_wait(barrier, 65 + extra)
     for e, source in ((1, visc), (0, s0)):
         start_x(e)
+    for copy in loads[4:]:
+        copy.wait()
     for e, source in ((1, visc), (0, s0)):
         stage_yz(e, source)
         start_yz(e)
+    weight_pairs = (
+        (lift_hbm, lift_w), (bias_hbm, bias_w), (gains_hbm, gains_w), (query_hbm, query_w),
+        (key_hbm, key_w), (value_hbm, value_w), (out_hbm, out_w), (up_hbm, up_w),
+        (down_hbm, down_w), (head_hbm, head_w),
+    )
+    weight_loads = []
+    for n, (src, dst) in enumerate(weight_pairs):
+        weight_loads.append(pltpu.make_async_copy(src, dst, weight_sem.at[n]))
+        weight_loads[-1].start()
+
 
     rows = iota((128, 128), 0)
     lanes = iota((128, 128), 1)
@@ -287,12 +301,12 @@
         paired = pool[x, pl.ds(0, 128, stride=2), :] + pool[x, pl.ds(1, 128, stride=2), :]
         filt[:, x, :] = dot_nt(pick, paired, HIGHEST)
 
-    slot = (gx // 4) * 8 + gy * 4 + lax.rem(gx, 4)
-
-    for tx, ty in others:
+    slot = lax.rem(gx // 4, 4) * 8 + gy * 4 + lax.rem(gx, 4)
+    for n, (tx, ty) in enumerate(others):
+        far = 1 if n < 32 else 0
         pltpu.make_async_remote_copy(
-            src_ref=filt.at[tx * 2 + ty], dst_ref=recv.at[slot], send_sem=a_send,
-            recv_sem=a_recv, device_id={"gx": tx, "gy": ty}, device_id_type=MESH,
+            src_ref=filt.at[tx * 2 + ty], dst_ref=recv.at[far * 32 + slot], send_sem=a_send,
+            recv_sem=a_recv.at[far], device_id={"gx": tx, "gy": ty}, device_id_type=MESH,
         ).start()
     recv[pl.ds(slot, 1)] = filt[pl.ds(plane, 1)]
 
@@ -306,14 +320,13 @@
         [jnp.broadcast_to(head_all[f : f + 1, :], (32, 128)) for f in range(4)], axis=0
     ).astype(BF16)
 
-    a_all = pltpu.make_async_remote_copy(
-        src_ref=filt.at[pl.ds(0, 63)], dst_ref=recv.at[pl.ds(0, 63)], send_sem=a_send,
-        recv_sem=a_recv, device_id={"gy": 1 - gy}, device_id_type=MESH,
-    )
-    a_all.wait_recv()
-
-    filtered = jnp.concatenate([recv[:, 0, :], recv[:, 1, :]], axis=0)
-    lane16 = lax.rem(lanes, 16)
+    a_near, a_far = (
+        pltpu.make_async_remote_copy(
+            src_ref=filt.at[pl.ds(0, n)], dst_ref=recv.at[pl.ds(0, n)], send_sem=a_send,
+            recv_sem=a_recv.at[far], device_id={"gy": 1 - gy}, device_id_type=MESH,
+        )
+        for far, n in ((0, 31), (1, 32))
+    )
 
     def block_weights(i):
         return (query_w[i], key_w[i], value_w[i], out_w[i], up_w[i], down_w[i])
@@ -321,34 +334,64 @@
     def gain(i):
         return gains_w[i : i + 1, :]
 
-    inputs = jnp.concatenate(
-        [jnp.where(lane16 == y, filtered, 0.0) for y in range(16)], axis=0
-    )
-    lifted = (
-        jnp.dot(inputs, lift_rows, precision=HIGHEST, preferred_element_type=F32) + bias_w[...]
-    )
-    features = gelu(rms(lifted, gain(0))).astype(BF16).astype(F32)
+    lift_parts = split(lift_rows, 3)
+    lift_pairs = [
+        jnp.concatenate([lift_parts[i], lift_parts[j]], axis=0)
+        for i, j in ((0, 0), (1, 1), (2, 0))
+    ]
+    lane16 = lax.rem(iota((64, 256), 1), 16)
+    own_y = [jnp.where(lane16 == y, 1.0, 0.0).astype(BF16) for y in range(16)]
+
+    def make_features(far):
+        cells = slice(far * 32, far * 32 + 32)
+        filtered = jnp.concatenate([recv[cells, 0, :], recv[cells, 1, :]], axis=0)
+        one, two, three = split(filtered, 3)
+        wide = jnp.concatenate([one, two], axis=1)
+        last = jnp.concatenate([one, three], axis=1)
+        wide = jnp.concatenate([wide * m for m in own_y], axis=0)
+        last = jnp.concatenate([last * m for m in own_y], axis=0)
+        lifted = dot(last, lift_pairs[2]) + dot(wide, lift_pairs[1]) + dot(wide, lift_pairs[0])
+        features = gelu(rms(lifted + bias_w[...], gain(0))).astype(BF16).astype(F32)
+        return features, project(features, gain(1), block_weights(0))
+
+    a_near.wait_recv()
+    near = make_features(0)
+    a_far.wait_recv()
+    far = make_features(1)
+    features, projected = (
+        jnp.concatenate(
+            [part[y * 64 : y * 64 + 64] for y in range(16) for part in halves], axis=0
+        )
+        for halves in zip(near, far)
+    )
     along_x = lax.rem(rows // 4, 2) == lax.rem(lanes // 4, 2)
-    result = mixer(features, along_x, (gain(1), gain(2)), block_weights(0))
+    result = mixer(features, projected, along_x, gain(2), block_weights(0))
     for y in range(16):
         part = result[y * 128 : y * 128 + 128].astype(F32)
         for c in range(16):
             hid[c, y] = part[c * 8 : c * 8 + 8]
 
     along_y = lax.rem(rows, 4) == lax.rem(lanes, 4)
-    result = mixer(
-        hid[...].reshape(2048, 128), along_y, (gain(3), gain(4)), block_weights(1)
-    )
-    final = rms(result.astype(F32), gain(5)).astype(BF16)
-    spread = dot_nt(final, head_rows)
     own_lane = lax.rem(lanes, 32) == lax.rem(rows // 4, 2) * 16 + rows // 8
-    for c in range(16):
-        part = jnp.where(own_lane, spread[c * 128 : c * 128 + 128], 0.0).reshape(16, 8, 128)
-        part = jnp.sum(part, axis=0)
-        logits = part + pltpu.roll(part, 4, 0)
-        coefficient = 0.05 + 0.45 * (1.0 / (1.0 + jnp.exp(-logits)))
-        for r in range(4):
-            cbuf[1 + c // 8 + 2 * (4 * (c % 8) + r)] = coefficient[r : r + 1, :]
+    z_hi = gx // 16
+
+    def finish(chunks):
+        lines = jnp.concatenate([hid[c].reshape(128, 128) for c in chunks], axis=0)
+        projected = project(lines, gain(3), block_weights(1))
+        result = mixer(lines, projected, along_y, gain(4), block_weights(1))
+        final = rms(result.astype(F32), gain(5)).astype(BF16)
+        spread = dot_nt(final, head_rows)
+        for n, c in enumerate(chunks):
+            part = jnp.where(own_lane, spread[n * 128 : n * 128 + 128], 0.0).reshape(16, 8, 128)
+            part = jnp.sum(part, axis=0)
+            logits = part + pltpu.roll(part, 4, 0)
+            coefficient = 0.05 + 0.45 * (1.0 / (1.0 + jnp.exp(-logits)))
+            half = 1 - z_hi if c >= 8 else z_hi
+            for r in range(4):
+                x = 2 * (4 * (c % 4) + r) + c // 4 % 2
+                cbuf[pl.ds(half * 32 + (1 + x), 1)] = coefficient[r : r + 1, :].reshape(1, 1, 128)
+
+    finish(range(16))
     cbuf[0] = cbuf[64]
     cbuf[65] = cbuf[1]
 
@@ -376,7 +419,7 @@
             send_edge(65, z_last, (others + [(gx, gy)])[half])
 
     ebuf[pl.ds(plane + 1, 1)] = cbuf[pl.ds(2 * gx, 4)].reshape(1, 4, 1, 128)
-    ebuf[66:72] = jnp.zeros((6, 4, 1, 128), F32)
+    ebuf[66:80] = jnp.zeros((14, 4, 1, 128), F32)
     b_all = pltpu.make_async_remote_copy(
         src_ref=ebuf.at[pl.ds(0, 63)], dst_ref=ebuf.at[pl.ds(0, 65)], send_sem=b_send,
         recv_sem=b_recv, device_id={"gy": 1 - gy}, device_id_type=MESH,
@@ -389,24 +432,28 @@
     along_y = jnp.where(same & (lax.rem(row, 32) == centre), 0.75, 0.0) + jnp.where(
         same & (lax.rem(row, 32) == other), 0.25, 0.0
     )
-    row, column = iota((72, 128), 0), iota((72, 128), 1)
+    row, column = iota((80, 128), 0), iota((80, 128), 1)
     centre = 1 + column // 2
     other = centre - 1 + 2 * lax.rem(column, 2)
     along_z = jnp.where(row == centre, 0.75, 0.0) + jnp.where(row == other, 0.25, 0.0)
+    along_y = jnp.concatenate([along_y.astype(BF16)] * 2, axis=0)
+    along_z = jnp.concatenate([along_z.astype(BF16)] * 2, axis=0)
     b_all.wait_recv()
     cells = [ebuf[:, x, 0, :] for x in range(4)]
     for x in range(4):
         centre, other = (1, 0, 1, 2, 2, 1, 2, 3)[2 * x : 2 * x + 2]
         mixed = 0.75 * cells[centre] + 0.25 * cells[other]
-        wide = jnp.dot(mixed, along_y, precision=HIGHEST, preferred_element_type=F32)
+        wide = dot(jnp.concatenate(split(mixed, 2), axis=1), along_y)
         full = lax.dot_general(
-            wide, along_z, (((0,), (0,)), ((), ())), precision=HIGHEST, preferred_element_type=F32
+            jnp.concatenate(split(wide, 2), axis=0), along_z, (((0,), (0,)), ((), ())),
+            preferred_element_type=F32,
         )
         eddy[:, x] = full.reshape(4, 32, 128)
     for e in range(4):
         for copy in copies[e]:
             copy.wait_send()
-    a_all.wait_send()
+    a_near.wait_send()
+    a_far.wait_send()
     b_all.wait_send()
 
     @pl.when((plane == 63) | (plane == 0))
@@ -454,7 +501,7 @@
             vmem((64, 2, 128), F32),
             vmem((16, 16, 8, 128), F32),
             vmem((66, 1, 128), F32),
-            vmem((72, 4, 1, 128), F32),
+            vmem((80, 4, 1, 128), F32),
         ]
         + [vmem(w.shape, w.dtype) for w in weights]
         + [
@@ -463,7 +510,7 @@
             DMA((4, 5)),
             DMA((4, 5)),
             DMA,
-            DMA,
+            DMA((2,)),
             DMA,
             DMA,
             DMA,

time: 63.2 us -> 60.3 us (0.954)
  Pallas kernels: 62.2 us -> 59.4 us
    pallas_call x1, Pallas kernels: 61.4 us -> 58.6 us  [per_device(): pl.pallas_call(main_kernel, out_shape=(vmem(block, F32), vmem(block, F32)...]
where the time goes in v3:
time: 60.3 us; the launch traced here: 60 us
  Pallas kernels  59.4 us (99%)
  between operations  0.64 us (1%)
    pallas_call x1, Pallas kernels, per_device(): pl.pallas_call(main_kernel, out_shape=(vmem(block, F32), vmem(block, F32)...  58.6 us

profile of v3, /device:TPU:1, one launch (start us, length us, event | category | flops | bytes accessed | tf_op | source)
XLA Modules:
  0.0 60.0 jit_solution(262604669841444010)
XLA Ops:
  0.6 58.6 %flow_and_columns.1 = (f32[4,4,32,128]{3,2,1,0:T(8,128)S(1)}, f32[4,4,32,128]{3,2,1,0:T(8,128)S(1)}) custom-call(f32[4,4,32,128]{3,2,1,0:T(8,128)} %state_hbm.1, f32[4,4,32,128]{3,2,1,0:T(8,128)} %visc_hbm.1, f32[8,128]{1,0:T(8,128)} %lift_hbm.1, f32[1,128]{1,0:T(1,128)} %bitcast.3, f32[6,128]{1,0:T(8,128)} %gains_hbm.1, bf16[2,128,128]{2,1,0:T(8,128)(2,1)} %query_hbm.1, ...), custom_call_target="tpu_custom_call" | custom-call | tf_op jit(solution)/shard_map/flow_and_columns/pallas_call | solution.py:483
  59.2 0.8 %store.1 = (f32[4,4,32,128]{3,2,1,0:T(8,128)}, f32[4,4,32,128]{3,2,1,0:T(8,128)}) custom-call(f32[4,4,32,128]{3,2,1,0:T(8,128)S(1)} %get-tuple-element.4.first, f32[4,4,32,128]{3,2,1,0:T(8,128)S(1)} %get-tuple-element.5.second), custom_call_target="tpu_custom_call" | custom-call | tf_op jit(solution)/shard_map/store/pallas_call | solution.py:523

commit v4 on v3

--- a/solution.py
+++ b/solution.py
@@ -52,16 +52,16 @@
     z, x, y = gx // 16, lax.rem(gx // 4, 4), lax.rem(gx, 4)
 
     def ring(place):
-        return [lax.rem(place + 2, 4), lax.rem(place + 1, 4), lax.rem(place + 3, 4), place]
+        return [(lax.rem(place + n, 4), min(n, 4 - n)) for n in (2, 1, 3, 0)]
 
     found = [
-        (tz * 16 + tx * 4 + ty, tc)
+        (dx + dy, tz * 16 + tx * 4 + ty, tc)
+        for tx, dx in ring(x)
+        for ty, dy in ring(y)
         for tz in (1 - z, z)
-        for tx in ring(x)
-        for ty in ring(y)
         for tc in (1 - gy, gy)
     ]
-    return found[:63]
+    return [(place, core) for _, place, core in sorted(found, key=lambda found: -found[0])]
 
 
 def project(flat, gain, weights):
@@ -113,16 +113,14 @@
 
     barrier = pltpu.get_barrier_semaphore()
     z_next, z_last = lax.rem(gz + 1, 4), lax.rem(gz + 3, 4)
-    for tx, ty in others:
-        pl.semaphore_signal(barrier, inc=1, device_id={"gx": tx, "gy": ty}, device_id_type=MESH)
-    for target in (z_next, z_last):
-        pl.semaphore_signal(barrier, inc=1, device_id={"gz": target}, device_id_type=MESH)
-    pl.semaphore_signal(
-        barrier, inc=1, device_id={"gx": 0, "gy": 0, "gz": z_next}, device_id_type=MESH
-    )
-    pl.semaphore_signal(
-        barrier, inc=1, device_id={"gx": 31, "gy": 1, "gz": z_last}, device_id_type=MESH
-    )
+    x_next, x_last = lax.rem(gx + 1, 32), lax.rem(gx + 31, 32)
+    z_kept = lax.rem(gz + 2, 4)
+    greeted = [{"gx": tx, "gy": ty, "gz": z_kept} for tx, ty in others]
+    greeted += [{"gx": x_next}, {"gx": x_last}, {"gz": z_next}, {"gz": z_last}, {"gy": 1 - gy}]
+    greeted += [{"gx": 31, "gy": 1, "gz": z_next}, {"gx": 0, "gy": 0, "gz": z_last}]
+    for device in greeted:
+        pl.semaphore_signal(barrier, inc=1, device_id=device, device_id_type=MESH)
+
     for copy in loads[:4]:
         copy.wait()
 
@@ -144,7 +142,6 @@
                 packed = jnp.where(lanes32 == 16 + j, block[:, 127:128], packed)
         zs[e] = packed
 
-    x_next, x_last = lax.rem(gx + 1, 32), lax.rem(gx + 31, 32)
 
     def face_copies(e):
         pairs = (
@@ -183,7 +180,7 @@
     stage_x(1, visc)
     stage_x(0, s0)
     extra = jnp.where(plane == 0, 64, 0) + jnp.where(plane == 63, 64, 0)
-    pl.semaphore_wait(barrier, 65 + extra)
+    pl.semaphore_wait(barrier, 69 + extra)
     for e, source in ((1, visc), (0, s0)):
         start_x(e)
     for copy in loads[4:]:
@@ -301,14 +298,15 @@
         paired = pool[x, pl.ds(0, 128, stride=2), :] + pool[x, pl.ds(1, 128, stride=2), :]
         filt[:, x, :] = dot_nt(pick, paired, HIGHEST)
 
-    slot = lax.rem(gx // 4, 4) * 8 + gy * 4 + lax.rem(gx, 4)
-    for n, (tx, ty) in enumerate(others):
-        far = 1 if n < 32 else 0
+    chip_x = lax.rem(gx // 4, 4)
+    late = 1 - lax.rem((chip_x + 1) // 2, 2)
+    slot = late * 32 + (gx // 16 * 2 + chip_x // 2) * 8 + gy * 4 + lax.rem(gx, 4)
+    for tx, ty in others:
         pltpu.make_async_remote_copy(
-            src_ref=filt.at[tx * 2 + ty], dst_ref=recv.at[far * 32 + slot], send_sem=a_send,
-            recv_sem=a_recv.at[far], device_id={"gx": tx, "gy": ty}, device_id_type=MESH,
+            src_ref=filt.at[tx * 2 + ty], dst_ref=recv.at[slot], send_sem=a_send,
+            recv_sem=a_recv.at[late], device_id={"gx": tx, "gy": ty, "gz": z_kept},
+            device_id_type=MESH,
         ).start()
-    recv[pl.ds(slot, 1)] = filt[pl.ds(plane, 1)]
 
     for copy in weight_loads:
         copy.wait()
@@ -320,12 +318,12 @@
         [jnp.broadcast_to(head_all[f : f + 1, :], (32, 128)) for f in range(4)], axis=0
     ).astype(BF16)
 
-    a_near, a_far = (
+    a_early, a_late = (
         pltpu.make_async_remote_copy(
-            src_ref=filt.at[pl.ds(0, n)], dst_ref=recv.at[pl.ds(0, n)], send_sem=a_send,
-            recv_sem=a_recv.at[far], device_id={"gy": 1 - gy}, device_id_type=MESH,
+            src_ref=filt.at[pl.ds(0, 32)], dst_ref=recv.at[pl.ds(0, 32)], send_sem=a_send,
+            recv_sem=a_recv.at[half], device_id={"gy": 1 - gy}, device_id_type=MESH,
         )
-        for far, n in ((0, 31), (1, 32))
+        for half in range(2)
     )
 
     def block_weights(i):
@@ -342,8 +340,8 @@
     lane16 = lax.rem(iota((64, 256), 1), 16)
     own_y = [jnp.where(lane16 == y, 1.0, 0.0).astype(BF16) for y in range(16)]
 
-    def make_features(far):
-        cells = slice(far * 32, far * 32 + 32)
+    def make_features(half):
+        cells = slice(half * 32, half * 32 + 32)
         filtered = jnp.concatenate([recv[cells, 0, :], recv[cells, 1, :]], axis=0)
         one, two, three = split(filtered, 3)
         wide = jnp.concatenate([one, two], axis=1)
@@ -354,15 +352,15 @@
         features = gelu(rms(lifted + bias_w[...], gain(0))).astype(BF16).astype(F32)
         return features, project(features, gain(1), block_weights(0))
 
-    a_near.wait_recv()
-    near = make_features(0)
-    a_far.wait_recv()
-    far = make_features(1)
+    a_early.wait_recv()
+    early = make_features(0)
+    a_late.wait_recv()
+    late = make_features(1)
     features, projected = (
         jnp.concatenate(
             [part[y * 64 : y * 64 + 64] for y in range(16) for part in halves], axis=0
         )
-        for halves in zip(near, far)
+        for halves in zip(early, late)
     )
     along_x = lax.rem(rows // 4, 2) == lax.rem(lanes // 4, 2)
     result = mixer(features, projected, along_x, gain(2), block_weights(0))
@@ -373,7 +371,6 @@
 
     along_y = lax.rem(rows, 4) == lax.rem(lanes, 4)
     own_lane = lax.rem(lanes, 32) == lax.rem(rows // 4, 2) * 16 + rows // 8
-    z_hi = gx // 16
 
     def finish(chunks):
         lines = jnp.concatenate([hid[c].reshape(128, 128) for c in chunks], axis=0)
@@ -386,10 +383,9 @@
             part = jnp.sum(part, axis=0)
             logits = part + pltpu.roll(part, 4, 0)
             coefficient = 0.05 + 0.45 * (1.0 / (1.0 + jnp.exp(-logits)))
-            half = 1 - z_hi if c >= 8 else z_hi
+            chip = c % 4 // 2 * 4 + (3 * (c % 2) if c >= 8 else 1 + c % 2)
             for r in range(4):
-                x = 2 * (4 * (c % 4) + r) + c // 4 % 2
-                cbuf[pl.ds(half * 32 + (1 + x), 1)] = coefficient[r : r + 1, :].reshape(1, 1, 128)
+                cbuf[1 + 2 * (4 * chip + r) + c // 4 % 2] = coefficient[r : r + 1, :]
 
     finish(range(16))
     cbuf[0] = cbuf[64]
@@ -403,25 +399,31 @@
                 device_id_type=MESH,
             ).start()
 
-    for half in (slice(0, 32), slice(32, 64)):
-        for tx, ty in others[half]:
-            pltpu.make_async_remote_copy(
-                src_ref=cbuf.at[pl.ds(2 * tx, 4)], dst_ref=ebuf.at[plane + 1], send_sem=b_send,
-                recv_sem=b_recv, device_id={"gx": tx, "gy": ty}, device_id_type=MESH,
-            ).start()
-
-        @pl.when(plane == 63)
-        def _(half=half):
-            send_edge(0, z_next, (others + [(gx, gy)])[half])
-
-        @pl.when(plane == 0)
-        def _(half=half):
-            send_edge(65, z_last, (others + [(gx, gy)])[half])
-
-    ebuf[pl.ds(plane + 1, 1)] = cbuf[pl.ds(2 * gx, 4)].reshape(1, 4, 1, 128)
+    @pl.when(plane == 63)
+    def _():
+        send_edge(0, z_last, others[:32])
+
+    @pl.when(plane == 0)
+    def _():
+        send_edge(65, z_next, others[:32])
+
+    for tx, ty in others:
+        pltpu.make_async_remote_copy(
+            src_ref=cbuf.at[pl.ds(2 * tx, 4)], dst_ref=ebuf.at[plane + 1], send_sem=b_send,
+            recv_sem=b_recv, device_id={"gx": tx, "gy": ty, "gz": z_kept}, device_id_type=MESH,
+        ).start()
+
+    @pl.when(plane == 63)
+    def _():
+        send_edge(0, z_last, others[32:])
+
+    @pl.when(plane == 0)
+    def _():
+        send_edge(65, z_next, others[32:])
+
     ebuf[66:80] = jnp.zeros((14, 4, 1, 128), F32)
     b_all = pltpu.make_async_remote_copy(
-        src_ref=ebuf.at[pl.ds(0, 63)], dst_ref=ebuf.at[pl.ds(0, 65)], send_sem=b_send,
+        src_ref=ebuf.at[pl.ds(0, 64)], dst_ref=ebuf.at[pl.ds(0, 66)], send_sem=b_send,
         recv_sem=b_recv, device_id={"gy": 1 - gy}, device_id_type=MESH,
     )
     row, column = rows, lanes
@@ -452,8 +454,8 @@
     for e in range(4):
         for copy in copies[e]:
             copy.wait_send()
-    a_near.wait_send()
-    a_far.wait_send()
+    a_early.wait_send()
+    a_late.wait_send()
     b_all.wait_send()
 
     @pl.when((plane == 63) | (plane == 0))

time: 60.3 us -> 59.2 us (0.982)
  Pallas kernels: 59.4 us -> 58.4 us
    pallas_call x1, Pallas kernels: 58.6 us -> 57.6 us  [per_device(): pl.pallas_call(main_kernel, out_shape=(vmem(block, F32), vmem(block, F32)...]
where the time goes in v4:
time: 59.2 us; the launch traced here: 59.1 us
  Pallas kernels  58.4 us (99%)
  between operations  0.64 us (1%)
    pallas_call x1, Pallas kernels, per_device(): pl.pallas_call(main_kernel, out_shape=(vmem(block, F32), vmem(block, F32)...  57.6 us

profile of v4, /device:TPU:1, one launch (start us, length us, event | category | flops | bytes accessed | tf_op | source)
XLA Modules:
  0.0 59.1 jit_solution(11360248432839188169)
XLA Ops:
  0.6 57.6 %flow_and_columns.1 = (f32[4,4,32,128]{3,2,1,0:T(8,128)S(1)}, f32[4,4,32,128]{3,2,1,0:T(8,128)S(1)}) custom-call(f32[4,4,32,128]{3,2,1,0:T(8,128)} %state_hbm.1, f32[4,4,32,128]{3,2,1,0:T(8,128)} %visc_hbm.1, f32[8,128]{1,0:T(8,128)} %lift_hbm.1, f32[1,128]{1,0:T(1,128)} %bitcast.3, f32[6,128]{1,0:T(8,128)} %gains_hbm.1, bf16[2,128,128]{2,1,0:T(8,128)(2,1)} %query_hbm.1, ...), custom_call_target="tpu_custom_call" | custom-call | tf_op jit(solution)/shard_map/flow_and_columns/pallas_call | solution.py:485
  58.3 0.8 %store.1 = (f32[4,4,32,128]{3,2,1,0:T(8,128)}, f32[4,4,32,128]{3,2,1,0:T(8,128)}) custom-call(f32[4,4,32,128]{3,2,1,0:T(8,128)S(1)} %get-tuple-element.4.first, f32[4,4,32,128]{3,2,1,0:T(8,128)S(1)} %get-tuple-element.5.second), custom_call_target="tpu_custom_call" | custom-call | tf_op jit(solution)/shard_map/store/pallas_call | solution.py:525

commit v5 on v4

--- a/solution.py
+++ b/solution.py
@@ -13,7 +13,6 @@
 F32 = jnp.float32
 BF16 = jnp.bfloat16
 DMA = pltpu.SemaphoreType.DMA
-HIGHEST = lax.Precision.HIGHEST
 
 
 def iota(shape, dim):
@@ -42,9 +41,9 @@
     return jnp.dot(left, right, preferred_element_type=F32)
 
 
-def dot_nt(left, right, precision=None):
+def dot_nt(left, right):
     return lax.dot_general(
-        left, right, (((1,), (1,)), ((), ())), precision=precision, preferred_element_type=F32
+        left, right, (((1,), (1,)), ((), ())), preferred_element_type=F32
     )
 
 
@@ -140,7 +139,7 @@
                 block = source[x, f]
                 packed = jnp.where(lanes32 == j, block[:, 0:1], packed)
                 packed = jnp.where(lanes32 == 16 + j, block[:, 127:128], packed)
-        zs[e] = packed
+        zs[e] = sum(pltpu.roll(packed[8 * g : 8 * g + 8], 32 * g, 1) for g in range(1, 4)) + packed[:8]
 
 
     def face_copies(e):
@@ -229,10 +228,9 @@
         def column(side, first):
             return jnp.concatenate(
                 [
-                    jnp.broadcast_to(
-                        zr[e, side, :, first + x * 4 + f : first + x * 4 + f + 1], (32, 128)
-                    )
+                    jnp.broadcast_to(zr[e, side, :, place : place + 1], (8, 128))
                     for f in range(4)
+                    for place in range(first + x * 4 + f, 128, 32)
                 ],
                 axis=0,
             )
@@ -291,16 +289,19 @@
         advance(e, source, combine, (0, 3))
 
     pick = jnp.where(iota((64, 128), 1) // 2 == iota((64, 128), 0), 0.125, 0.0)
+    pick = jnp.concatenate([pick.astype(BF16)] * 3, axis=1)
     for x in range(2):
         one, two = (s3[:, 2 * x + i].reshape(128, 128) for i in range(2))
         pool[x, 0:128] = one + two
         pool[x, 128:256] = one * one + two * two
         paired = pool[x, pl.ds(0, 128, stride=2), :] + pool[x, pl.ds(1, 128, stride=2), :]
-        filt[:, x, :] = dot_nt(pick, paired, HIGHEST)
-
-    chip_x = lax.rem(gx // 4, 4)
-    late = 1 - lax.rem((chip_x + 1) // 2, 2)
-    slot = late * 32 + (gx // 16 * 2 + chip_x // 2) * 8 + gy * 4 + lax.rem(gx, 4)
+        filt[:, x, :] = dot_nt(pick, jnp.concatenate(split(paired, 3), axis=1))
+
+    z_hi, chip_x, chip_y = gx // 16, lax.rem(gx // 4, 4), lax.rem(gx, 4)
+    outer = 1 - lax.rem((chip_x + 1) // 2, 2)
+    late = outer * (1 - lax.rem(chip_x // 2 + chip_y // 2, 2))
+    group = (1 - late) * (z_hi * 3 + (1 - outer) * (chip_x - 1) + outer * 2) + late * (6 + z_hi)
+    slot = group * 8 + gy * 4 + lax.rem(chip_y + 2 * outer * (1 - late), 4)
     for tx, ty in others:
         pltpu.make_async_remote_copy(
             src_ref=filt.at[tx * 2 + ty], dst_ref=recv.at[slot], send_sem=a_send,
@@ -320,10 +321,10 @@
 
     a_early, a_late = (
         pltpu.make_async_remote_copy(
-            src_ref=filt.at[pl.ds(0, 32)], dst_ref=recv.at[pl.ds(0, 32)], send_sem=a_send,
-            recv_sem=a_recv.at[half], device_id={"gy": 1 - gy}, device_id_type=MESH,
+            src_ref=filt.at[pl.ds(0, n)], dst_ref=recv.at[pl.ds(0, n)], send_sem=a_send,
+            recv_sem=a_recv.at[part], device_id={"gy": 1 - gy}, device_id_type=MESH,
         )
-        for half in range(2)
+        for part, n in ((0, 48), (1, 16))
     )
 
     def block_weights(i):
@@ -337,30 +338,35 @@
         jnp.concatenate([lift_parts[i], lift_parts[j]], axis=0)
         for i, j in ((0, 0), (1, 1), (2, 0))
     ]
-    lane16 = lax.rem(iota((64, 256), 1), 16)
+    lane16 = lax.rem(iota((32, 256), 1), 16)
     own_y = [jnp.where(lane16 == y, 1.0, 0.0).astype(BF16) for y in range(16)]
 
-    def make_features(half):
-        cells = slice(half * 32, half * 32 + 32)
+    def make_features(cells):
         filtered = jnp.concatenate([recv[cells, 0, :], recv[cells, 1, :]], axis=0)
+        repeat = filtered.shape[0] // 32
         one, two, three = split(filtered, 3)
         wide = jnp.concatenate([one, two], axis=1)
         last = jnp.concatenate([one, three], axis=1)
-        wide = jnp.concatenate([wide * m for m in own_y], axis=0)
-        last = jnp.concatenate([last * m for m in own_y], axis=0)
+        wide = jnp.concatenate([wide * jnp.concatenate([m] * repeat, axis=0) for m in own_y], axis=0)
+        last = jnp.concatenate([last * jnp.concatenate([m] * repeat, axis=0) for m in own_y], axis=0)
         lifted = dot(last, lift_pairs[2]) + dot(wide, lift_pairs[1]) + dot(wide, lift_pairs[0])
         features = gelu(rms(lifted + bias_w[...], gain(0))).astype(BF16).astype(F32)
         return features, project(features, gain(1), block_weights(0))
 
     a_early.wait_recv()
-    early = make_features(0)
+    early = make_features(slice(0, 48))
     a_late.wait_recv()
-    late = make_features(1)
+    last = make_features(slice(48, 64))
     features, projected = (
         jnp.concatenate(
-            [part[y * 64 : y * 64 + 64] for y in range(16) for part in halves], axis=0
+            [
+                part[y * n : y * n + n]
+                for y in range(16)
+                for part, n in zip(parts, (96, 32))
+            ],
+            axis=0,
         )
-        for halves in zip(early, late)
+        for parts in zip(early, last)
     )
     along_x = lax.rem(rows // 4, 2) == lax.rem(lanes // 4, 2)
     result = mixer(features, projected, along_x, gain(2), block_weights(0))
@@ -383,9 +389,15 @@
             part = jnp.sum(part, axis=0)
             logits = part + pltpu.roll(part, 4, 0)
             coefficient = 0.05 + 0.45 * (1.0 / (1.0 + jnp.exp(-logits)))
-            chip = c % 4 // 2 * 4 + (3 * (c % 2) if c >= 8 else 1 + c % 2)
+            parity, group = (c // 6, c % 6) if c < 12 else (c % 4 // 2, 6 + c % 2)
             for r in range(4):
-                cbuf[1 + 2 * (4 * chip + r) + c // 4 % 2] = coefficient[r : r + 1, :]
+                if group >= 6:
+                    place = (group - 6) * 16 + (0, 1, 14, 15)[r]
+                else:
+                    place = group // 3 * 16 + ((4, 5, 6, 7), (8, 9, 10, 11), (2, 3, 12, 13))[
+                        group % 3
+                    ][r]
+                cbuf[1 + 2 * place + parity] = coefficient[r : r + 1, :]
 
     finish(range(16))
     cbuf[0] = cbuf[64]
@@ -496,8 +508,8 @@
             vmem((4, 2, 4, 32, 128), BF16),
             vmem((4, 2, 16, 128), F32),
             vmem((4, 2, 16, 128), F32),
-            vmem((4, 32, 128), F32),
-            vmem((4, 2, 32, 128), F32),
+            vmem((4, 8, 128), F32),
+            vmem((4, 2, 8, 128), F32),
             vmem((2, 256, 128), F32),
             vmem((64, 2, 128), F32),
             vmem((64, 2, 128), F32),

time: 59.2 us -> 58.7 us (level)
  no operation moved by 1% of the time
where the time goes in v5:
time: 58.7 us; the launch traced here: 58.6 us
  Pallas kernels  58 us (99%)
  between operations  0.64 us (1%)
    pallas_call x1, Pallas kernels, per_device(): pl.pallas_call(main_kernel, out_shape=(vmem(block, F32), vmem(block, F32)...  57.2 us

profile of v5, /device:TPU:1, one launch (start us, length us, event | category | flops | bytes accessed | tf_op | source)
XLA Modules:
  0.0 58.6 jit_solution(5621669050482929280)
XLA Ops:
  0.6 57.2 %flow_and_columns.1 = (f32[4,4,32,128]{3,2,1,0:T(8,128)S(1)}, f32[4,4,32,128]{3,2,1,0:T(8,128)S(1)}) custom-call(f32[4,4,32,128]{3,2,1,0:T(8,128)} %state_hbm.1, f32[4,4,32,128]{3,2,1,0:T(8,128)} %visc_hbm.1, f32[8,128]{1,0:T(8,128)} %lift_hbm.1, f32[1,128]{1,0:T(1,128)} %bitcast.3, f32[6,128]{1,0:T(8,128)} %gains_hbm.1, bf16[2,128,128]{2,1,0:T(8,128)(2,1)} %query_hbm.1, ...), custom_call_target="tpu_custom_call" | custom-call | tf_op jit(solution)/shard_map/flow_and_columns/pallas_call | solution.py:497
  57.8 0.8 %store.1 = (f32[4,4,32,128]{3,2,1,0:T(8,128)}, f32[4,4,32,128]{3,2,1,0:T(8,128)}) custom-call(f32[4,4,32,128]{3,2,1,0:T(8,128)S(1)} %get-tuple-element.4.first, f32[4,4,32,128]{3,2,1,0:T(8,128)S(1)} %get-tuple-element.5.second), custom_call_target="tpu_custom_call" | custom-call | tf_op jit(solution)/shard_map/store/pallas_call | solution.py:537
